TPU v7x, 32 devices: a whole 2x2x4 slice. The times are simulated.
32 devices in a mesh: rep: 4 (over y, core), shard: 8 (over z, x).
Axes of the slice: x: 2, y: 2, z: 4, core: 2. Of those that a mesh axis runs over, the one named last changes fastest.
Arguments:
- layer_input: bfloat16 [32, 197, 768], P(('rep', 'shard')), may hold values from -6 to 6
- cotangent: bfloat16 [32, 197, 768], P(('rep', 'shard')), may hold values from -6 to 6
- live: int32 [32], P(('rep', 'shard')), may hold values 0 or 1
- first_gain: bfloat16 [768], P('shard'), may hold values from 0.099609375 to 1.8984375
- first_bias: bfloat16 [768], P('shard'), may hold values from -3 to 3
- qkv_weight: bfloat16 [768, 2304], P('shard'), may hold values from -0.21875 to 0.21875
- query_bias: bfloat16 [768], P('shard'), may hold values from -3 to 3
- value_bias: bfloat16 [768], P('shard'), may hold values from -3 to 3
- out_weight: bfloat16 [768, 768], P('shard'), may hold values from -1.5 to 1.5
- out_bias: bfloat16 [768], P('shard'), may hold values from -3 to 3
- second_gain: bfloat16 [768], P('shard'), may hold values from 0.099609375 to 1.8984375
- second_bias: bfloat16 [768], P('shard'), may hold values from -3 to 3
- up_weight: bfloat16 [768, 3072], P('shard'), may hold values from -0.21875 to 0.21875
- up_bias: bfloat16 [3072], P('shard'), may hold values from -3 to 3
- down_weight: bfloat16 [3072, 768], P('shard'), may hold values from -0.109375 to 0.109375
- down_bias: bfloat16 [768], P('shard'), may hold values from -3 to 3
Outputs:
- output: bfloat16 [32, 197, 768], P(('rep', 'shard'))
- input_grad: bfloat16 [32, 197, 768], P(('rep', 'shard'))
- first_gain_grad: float32 [768], P('shard')
- first_bias_grad: float32 [768], P('shard')
- qkv_weight_grad: float32 [768, 2304], P('shard')
- query_bias_grad: float32 [768], P('shard')
- value_bias_grad: float32 [768], P('shard')
- out_weight_grad: float32 [768, 768], P('shard')
- out_bias_grad: float32 [768], P('shard')
- second_gain_grad: float32 [768], P('shard')
- second_bias_grad: float32 [768], P('shard')
- up_weight_grad: float32 [768, 3072], P('shard')
- up_bias_grad: float32 [3072], P('shard')
- down_weight_grad: float32 [3072, 768], P('shard')
- down_bias_grad: float32 [768], P('shard')
All inputs are finite; a program needn't handle non-finite values. No bound on the sum of `live` on one device may be relied on, other than what follows from the above.
Results may differ from a plain program's by a relative error of at most 0.014.
Values may be sent and summed in bfloat16 or wider, within the bound.
A program may use at most 128 MiB of HBM per device.

v0:
```python
import jax
import jax.numpy as jnp
from jax import lax
from jax.sharding import PartitionSpec as P

HEAD_DIM = 64
norm_eps = 1e-06
root_half = 0.7071067811865476
density_coef = 0.3989422804014327


def matmul(operand, factor):
    flat = operand.reshape(-1, operand.shape[-1])
    product = jnp.dot(flat, factor, preferred_element_type=jnp.float32)
    return product.reshape(operand.shape[:-1] + (factor.shape[-1],))


def outer_product(operand, factor):
    return jnp.dot(
        operand.reshape(-1, operand.shape[-1]).T,
        factor.reshape(-1, factor.shape[-1]),
        preferred_element_type=jnp.float32,
    )


def batched(form, operand, factor):
    return jnp.einsum(form, operand, factor, preferred_element_type=jnp.float32)


def layer_norm(values, norm_gain, norm_bias):
    average = jnp.mean(values, axis=-1, keepdims=True)
    centred = values - average
    spread = jnp.mean(centred * centred, axis=-1, keepdims=True)
    inv_std = lax.rsqrt(spread + norm_eps)
    hat_vals = centred * inv_std
    return (
        hat_vals * norm_gain.astype(jnp.float32) + norm_bias.astype(jnp.float32),
        hat_vals,
        inv_std,
    )


def norm_back(incoming, hat_vals, inv_std, norm_gain):
    scaled = incoming * norm_gain.astype(jnp.float32)
    return inv_std * (
        scaled
        - jnp.mean(scaled, axis=-1, keepdims=True)
        - hat_vals * jnp.mean(scaled * hat_vals, axis=-1, keepdims=True)
    )


def forward_pass(params, layer_input, live):
    (
        first_gain,
        first_bias,
        qkv_weight,
        query_bias,
        value_bias,
        out_weight,
        out_bias,
        second_gain,
        second_bias,
        up_weight,
        up_bias,
        down_weight,
        down_bias,
    ) = params
    images, length, model_width = layer_input.shape
    head_count = model_width // HEAD_DIM
    score_scale = HEAD_DIM ** (-0.5)
    stream = layer_input.astype(jnp.float32)
    normed, first_hat, first_inv = layer_norm(stream, first_gain, first_bias)
    normed = normed.astype(jnp.bfloat16)
    projected = matmul(normed, qkv_weight)
    shape_heads = (images, length, head_count, HEAD_DIM)
    queries = (
        (projected[..., :model_width] + query_bias.astype(jnp.float32))
        .astype(jnp.bfloat16)
        .reshape(shape_heads)
    )
    key_rows = (
        projected[..., model_width : 2 * model_width].astype(jnp.bfloat16).reshape(shape_heads)
    )
    values = (
        (projected[..., 2 * model_width :] + value_bias.astype(jnp.float32))
        .astype(jnp.bfloat16)
        .reshape(shape_heads)
    )
    scores = batched("bqhd,bkhd->bhqk", queries, key_rows) * score_scale
    log_total = jnp.log(jnp.sum(jnp.exp(scores), axis=-1, keepdims=True))
    weights = jnp.exp(scores - log_total).astype(jnp.bfloat16)
    attended = (
        batched("bhqk,bkhd->bqhd", weights, values)
        .reshape(images, length, model_width)
        .astype(jnp.bfloat16)
    )
    middle = stream + matmul(attended, out_weight) + out_bias.astype(jnp.float32)
    second_normed, second_hat, second_inv = layer_norm(middle, second_gain, second_bias)
    second_normed = second_normed.astype(jnp.bfloat16)
    hidden_pre = matmul(second_normed, up_weight) + up_bias.astype(jnp.float32)
    normal_cdf = 0.5 * (1.0 + lax.erf(hidden_pre * root_half))
    hidden = (hidden_pre * normal_cdf).astype(jnp.bfloat16)
    result = middle + matmul(hidden, down_weight) + down_bias.astype(jnp.float32)
    image_mask = live.astype(jnp.float32)[:, None, None]
    output = (result * image_mask).astype(jnp.bfloat16)
    saved = (
        normed,
        first_hat,
        first_inv,
        queries,
        key_rows,
        values,
        log_total,
        attended,
        second_normed,
        second_hat,
        second_inv,
        hidden_pre,
        normal_cdf,
        hidden,
        image_mask,
    )
    return (output, saved)


def backward_pass(params, saved, cotangent):
    (
        first_gain,
        first_bias,
        qkv_weight,
        query_bias,
        value_bias,
        out_weight,
        out_bias,
        second_gain,
        second_bias,
        up_weight,
        up_bias,
        down_weight,
        down_bias,
    ) = params
    (
        normed,
        first_hat,
        first_inv,
        queries,
        key_rows,
        values,
        log_total,
        attended,
        second_normed,
        second_hat,
        second_inv,
        hidden_pre,
        normal_cdf,
        hidden,
        image_mask,
    ) = saved
    images, length, head_count, head_width = queries.shape
    flat_shape = (images, length, head_count * head_width)
    score_scale = HEAD_DIM ** (-0.5)
    upstream = cotangent.astype(jnp.float32) * image_mask
    upstream_low = upstream.astype(jnp.bfloat16)
    down_weight_grad = outer_product(hidden, upstream_low)
    down_bias_grad = jnp.sum(upstream, axis=(0, 1))
    hidden_grad = matmul(upstream_low, down_weight.T)
    density = jnp.exp(-0.5 * hidden_pre * hidden_pre) * density_coef
    pre_grad = hidden_grad * (normal_cdf + hidden_pre * density)
    pre_low = pre_grad.astype(jnp.bfloat16)
    up_weight_grad = outer_product(second_normed, pre_low)
    up_bias_grad = jnp.sum(pre_grad, axis=(0, 1))
    second_in = matmul(pre_low, up_weight.T)
    second_gain_grad = jnp.sum(second_in * second_hat, axis=(0, 1))
    second_bias_grad = jnp.sum(second_in, axis=(0, 1))
    middle_grad = upstream + norm_back(second_in, second_hat, second_inv, second_gain)
    middle_low = middle_grad.astype(jnp.bfloat16)
    out_weight_grad = outer_product(attended, middle_low)
    out_bias_grad = jnp.sum(middle_grad, axis=(0, 1))
    attended_grad = matmul(middle_low, out_weight.T).astype(jnp.bfloat16).reshape(queries.shape)
    again_scores = batched("bqhd,bkhd->bhqk", queries, key_rows) * score_scale
    probs = jnp.exp(again_scores - log_total)
    probs_low = probs.astype(jnp.bfloat16)
    value_grad = batched("bhqk,bqhd->bkhd", probs_low, attended_grad)
    prob_grad = batched("bqhd,bkhd->bhqk", attended_grad, values)
    score_grad = (
        probs * (prob_grad - jnp.sum(probs * prob_grad, axis=-1, keepdims=True)) * score_scale
    ).astype(jnp.bfloat16)
    query_grad = batched("bhqk,bkhd->bqhd", score_grad, key_rows).reshape(flat_shape)
    key_grad = batched("bhqk,bqhd->bkhd", score_grad, queries).reshape(flat_shape)
    value_grad = value_grad.reshape(flat_shape)
    joined = jnp.concatenate([query_grad, key_grad, value_grad], axis=-1).astype(jnp.bfloat16)
    qkv_weight_grad = outer_product(normed, joined)
    query_bias_grad = jnp.sum(query_grad, axis=(0, 1))
    value_bias_grad = jnp.sum(value_grad, axis=(0, 1))
    first_in = matmul(joined, qkv_weight.T)
    first_gain_grad = jnp.sum(first_in * first_hat, axis=(0, 1))
    first_bias_grad = jnp.sum(first_in, axis=(0, 1))
    middle_grad = middle_grad + norm_back(first_in, first_hat, first_inv, first_gain)
    input_grad = middle_grad.astype(jnp.bfloat16)
    grads = (
        first_gain_grad,
        first_bias_grad,
        qkv_weight_grad,
        query_bias_grad,
        value_bias_grad,
        out_weight_grad,
        out_bias_grad,
        second_gain_grad,
        second_bias_grad,
        up_weight_grad,
        up_bias_grad,
        down_weight_grad,
        down_bias_grad,
    )
    return (input_grad, grads)


def per_device(
    layer_input,
    cotangent,
    live,
    first_gain,
    first_bias,
    qkv_weight,
    query_bias,
    value_bias,
    out_weight,
    out_bias,
    second_gain,
    second_bias,
    up_weight,
    up_bias,
    down_weight,
    down_bias,
):
    gathered = (
        lax.all_gather(first_gain, "shard", axis=0, tiled=True),
        lax.all_gather(first_bias, "shard", axis=0, tiled=True),
        lax.all_gather(qkv_weight, "shard", axis=0, tiled=True),
        lax.all_gather(query_bias, "shard", axis=0, tiled=True),
        lax.all_gather(value_bias, "shard", axis=0, tiled=True),
        lax.all_gather(out_weight, "shard", axis=0, tiled=True),
        lax.all_gather(out_bias, "shard", axis=0, tiled=True),
        lax.all_gather(second_gain, "shard", axis=0, tiled=True),
        lax.all_gather(second_bias, "shard", axis=0, tiled=True),
        lax.all_gather(up_weight, "shard", axis=0, tiled=True),
        lax.all_gather(up_bias, "shard", axis=0, tiled=True),
        lax.all_gather(down_weight, "shard", axis=0, tiled=True),
        lax.all_gather(down_bias, "shard", axis=0, tiled=True),
    )
    output, saved = forward_pass(gathered, layer_input, live)
    backward_params = (
        lax.all_gather(first_gain, "shard", axis=0, tiled=True),
        lax.all_gather(first_bias, "shard", axis=0, tiled=True),
        lax.all_gather(qkv_weight, "shard", axis=0, tiled=True),
        lax.all_gather(query_bias, "shard", axis=0, tiled=True),
        lax.all_gather(value_bias, "shard", axis=0, tiled=True),
        lax.all_gather(out_weight, "shard", axis=0, tiled=True),
        lax.all_gather(out_bias, "shard", axis=0, tiled=True),
        lax.all_gather(second_gain, "shard", axis=0, tiled=True),
        lax.all_gather(second_bias, "shard", axis=0, tiled=True),
        lax.all_gather(up_weight, "shard", axis=0, tiled=True),
        lax.all_gather(up_bias, "shard", axis=0, tiled=True),
        lax.all_gather(down_weight, "shard", axis=0, tiled=True),
        lax.all_gather(down_bias, "shard", axis=0, tiled=True),
    )
    input_grad, grads = backward_pass(backward_params, saved, cotangent)
    g00, g01, g02, g03, g04, g05, g06, g07, g08, g09, g10, g11, g12 = grads
    owned = (
        lax.psum_scatter(g00, "shard", scatter_dimension=0, tiled=True),
        lax.psum_scatter(g01, "shard", scatter_dimension=0, tiled=True),
        lax.psum_scatter(g02, "shard", scatter_dimension=0, tiled=True),
        lax.psum_scatter(g03, "shard", scatter_dimension=0, tiled=True),
        lax.psum_scatter(g04, "shard", scatter_dimension=0, tiled=True),
        lax.psum_scatter(g05, "shard", scatter_dimension=0, tiled=True),
        lax.psum_scatter(g06, "shard", scatter_dimension=0, tiled=True),
        lax.psum_scatter(g07, "shard", scatter_dimension=0, tiled=True),
        lax.psum_scatter(g08, "shard", scatter_dimension=0, tiled=True),
        lax.psum_scatter(g09, "shard", scatter_dimension=0, tiled=True),
        lax.psum_scatter(g10, "shard", scatter_dimension=0, tiled=True),
        lax.psum_scatter(g11, "shard", scatter_dimension=0, tiled=True),
        lax.psum_scatter(g12, "shard", scatter_dimension=0, tiled=True),
    )
    o00, o01, o02, o03, o04, o05, o06, o07, o08, o09, o10, o11, o12 = owned
    quarter = (
        lax.psum_scatter(o00.astype(jnp.bfloat16), "rep", scatter_dimension=0, tiled=True).astype(
            jnp.float32
        ),
        lax.psum_scatter(o01.astype(jnp.bfloat16), "rep", scatter_dimension=0, tiled=True).astype(
            jnp.float32
        ),
        lax.psum_scatter(o02.astype(jnp.bfloat16), "rep", scatter_dimension=0, tiled=True).astype(
            jnp.float32
        ),
        lax.psum_scatter(o03.astype(jnp.bfloat16), "rep", scatter_dimension=0, tiled=True).astype(
            jnp.float32
        ),
        lax.psum_scatter(o04.astype(jnp.bfloat16), "rep", scatter_dimension=0, tiled=True).astype(
            jnp.float32
        ),
        lax.psum_scatter(o05.astype(jnp.bfloat16), "rep", scatter_dimension=0, tiled=True).astype(
            jnp.float32
        ),
        lax.psum_scatter(o06.astype(jnp.bfloat16), "rep", scatter_dimension=0, tiled=True).astype(
            jnp.float32
        ),
        lax.psum_scatter(o07.astype(jnp.bfloat16), "rep", scatter_dimension=0, tiled=True).astype(
            jnp.float32
        ),
        lax.psum_scatter(o08.astype(jnp.bfloat16), "rep", scatter_dimension=0, tiled=True).astype(
            jnp.float32
        ),
        lax.psum_scatter(o09.astype(jnp.bfloat16), "rep", scatter_dimension=0, tiled=True).astype(
            jnp.float32
        ),
        lax.psum_scatter(o10.astype(jnp.bfloat16), "rep", scatter_dimension=0, tiled=True).astype(
            jnp.float32
        ),
        lax.psum_scatter(o11.astype(jnp.bfloat16), "rep", scatter_dimension=0, tiled=True).astype(
            jnp.float32
        ),
        lax.psum_scatter(o12.astype(jnp.bfloat16), "rep", scatter_dimension=0, tiled=True).astype(
            jnp.float32
        ),
    )
    q00, q01, q02, q03, q04, q05, q06, q07, q08, q09, q10, q11, q12 = quarter
    summed = (
        lax.all_gather(q00.astype(jnp.bfloat16), "rep", axis=0, tiled=True).astype(q00.dtype),
        lax.all_gather(q01.astype(jnp.bfloat16), "rep", axis=0, tiled=True).astype(q01.dtype),
        lax.all_gather(q02.astype(jnp.bfloat16), "rep", axis=0, tiled=True).astype(q02.dtype),
        lax.all_gather(q03.astype(jnp.bfloat16), "rep", axis=0, tiled=True).astype(q03.dtype),
        lax.all_gather(q04.astype(jnp.bfloat16), "rep", axis=0, tiled=True).astype(q04.dtype),
        lax.all_gather(q05.astype(jnp.bfloat16), "rep", axis=0, tiled=True).astype(q05.dtype),
        lax.all_gather(q06.astype(jnp.bfloat16), "rep", axis=0, tiled=True).astype(q06.dtype),
        lax.all_gather(q07.astype(jnp.bfloat16), "rep", axis=0, tiled=True).astype(q07.dtype),
        lax.all_gather(q08.astype(jnp.bfloat16), "rep", axis=0, tiled=True).astype(q08.dtype),
        lax.all_gather(q09.astype(jnp.bfloat16), "rep", axis=0, tiled=True).astype(q09.dtype),
        lax.all_gather(q10.astype(jnp.bfloat16), "rep", axis=0, tiled=True).astype(q10.dtype),
        lax.all_gather(q11.astype(jnp.bfloat16), "rep", axis=0, tiled=True).astype(q11.dtype),
        lax.all_gather(q12.astype(jnp.bfloat16), "rep", axis=0, tiled=True).astype(q12.dtype),
    )
    return (
        output,
        input_grad,
        summed[0],
        summed[1],
        summed[2],
        summed[3],
        summed[4],
        summed[5],
        summed[6],
        summed[7],
        summed[8],
        summed[9],
        summed[10],
        summed[11],
        summed[12],
    )


def solution(mesh):
    placed = (
        P(("rep", "shard"), None, None),
        P(("rep", "shard"), None, None),
        P(("rep", "shard")),
        P("shard"),
        P("shard"),
        P("shard", None),
        P("shard"),
        P("shard"),
        P("shard", None),
        P("shard"),
        P("shard"),
        P("shard"),
        P("shard", None),
        P("shard"),
        P("shard", None),
        P("shard"),
    )
    return jax.shard_map(
        per_device,
        mesh=mesh,
        in_specs=placed,
        out_specs=(
            P(("rep", "shard"), None, None),
            P(("rep", "shard"), None, None),
            P("shard"),
            P("shard"),
            P("shard", None),
            P("shard"),
            P("shard"),
            P("shard", None),
            P("shard"),
            P("shard"),
            P("shard"),
            P("shard", None),
            P("shard"),
            P("shard", None),
            P("shard"),
        ),
        check_vma=False,
    )
```

profile of v0, /device:TPU:0, one launch (start us, length us, event | category | flops | bytes accessed | tf_op | source)
XLA Modules:
  0.0 931.1 jit_solution(7860005917995283044)
XLA Ops:
  10.0 1.3 fusion.110
  12.0 0.8 dynamic-update-slice.1
  12.9 0.8 dynamic-update-slice
  13.7 0.8 dynamic-update-slice.2
  14.6 0.8 dynamic-update-slice.3
  15.4 0.8 dynamic-update-slice.4
  16.2 0.8 dynamic-update-slice.7
  17.1 0.8 dynamic-update-slice.6
  17.9 0.8 dynamic-update-slice.5
  18.7 40.4 %all-reduce.36 = (bf16[768]{0:T(1024)(128)(2,1)S(1)}, bf16[768]{0:T(1024)(128)(2,1)S(1)}, bf16[768]{0:T(1024)(128)(2,1)S(1)}, bf16[768]{0:T(1024)(128)(2,1)S(1)}...) all-reduce(bf16[768]{0:T(1024)(128)(2,1)S(1)} %dynamic-update-slice, ...), channel_id=1, replica_groups=mesh['rep'=4,'shard'=8] {'shard'}, use_global_device_ids=true, to_apply=%add.1 | all-reduce | flops 6144 | bytes 24576
  60.5 26.5 %all-gather = bf16[8,1,384]{2,1,0:T(2,128)(2,1)S(1)} all-gather(bf16[1,1,384]{2,1,0:T(2,128)(2,1)S(1)} %reshape.374), channel_id=1, replica_groups=mesh['rep'=4,'shard'=8] {'shard'}, dimensions={0}, use_global_device_ids=true | all-gather | bytes 6912 | tf_op jit(solution)/shard_map/all_gather | solution.py:247
  87.0 1.1 convert_reduce_fusion
  88.4 3.0 convolution_bitcast_fusion
  91.4 0.8 slice.23
  92.2 0.9 copy.51
  93.1 0.9 copy.52
  94.0 1.1 copy.53
  95.2 1.7 fusion.118
  96.9 2.3 convolution_convert_fusion
  99.2 21.3 %all-gather.8.cloned.1.call-done = bf16[768,768]{1,0:T(8,128)(2,1)} async-done(((bf16[96,768]{1,0:T(8,128)(2,1)}), bf16[768,768]{1,0:T(8,128)(2,1)}) %all-gather.8.cloned.1.call-update) | async-done | bytes 1179664 | tf_op jit(solution)/shard_map/all_gather | solution.py:242
  120.5 1.8 fusion.112
  122.5 78.2 %all-gather.10.cloned.1.call-done = bf16[768,3072]{1,0:T(8,128)(2,1)} async-done(((bf16[96,3072]{1,0:T(8,128)(2,1)}), bf16[768,3072]{1,0:T(8,128)(2,1)}) %all-gather.10.cloned.1.call-update) | async-done | bytes 4718608 | tf_op jit(solution)/shard_map/all_gather | solution.py:246
  200.7 3.6 convolution_add_fusion
  204.3 76.2 %all-gather.12.cloned.1.call-done = bf16[3072,768]{1,0:T(8,128)(2,1)} async-done(((bf16[384,768]{1,0:T(8,128)(2,1)}), bf16[3072,768]{1,0:T(8,128)(2,1)}) %all-gather.12.cloned.1.call-update) | async-done | bytes 4718608 | tf_op jit(solution)/shard_map/all_gather | solution.py:248
  280.5 4.3 fusion.117
  284.9 1.8 fusion.52
  287.2 0.8 copy-done.1
  288.0 1.9 fusion.77
  290.2 3.9 fusion.6
  294.1 2.7 convolution_convert_fusion.1
  296.8 1.9 copy.55
  298.7 4.3 fusion.108
  303.0 3.1 fusion.119
  306.1 5.6 fusion.23
  311.7 5.5 fusion.109
  317.2 5.4 fusion.64
  322.7 6.5 fusion.56
  329.3 5.6 fusion.80
  335.0 23.1 %reduce-scatter.13.cloned.1.call-done = f32[96,768]{1,0:T(8,128)} async-done(((f32[768,768]{1,0:T(8,128)}), f32[96,768]{1,0:T(8,128)}) %reduce-scatter.13.cloned.1.call-update) | async-done | bytes 294928 | tf_op jit(solution)/shard_map/reduce_scatter | solution.py:275
  358.1 1.6 convert_element_type.249
  359.8 130.2 %reduce-scatter.9.cloned.1.call-done = f32[96,2304]{1,0:T(8,128)} async-done(((f32[768,2304]{1,0:T(8,128)}), f32[96,2304]{1,0:T(8,128)}) %reduce-scatter.9.cloned.1.call-update) | async-done | bytes 884752 | tf_op jit(solution)/shard_map/reduce_scatter | solution.py:272
  490.0 2.0 convert_element_type.243
  492.1 162.8 %reduce-scatter.17.cloned.1.call-done = f32[96,3072]{1,0:T(8,128)} async-done(((f32[768,3072]{1,0:T(8,128)}), f32[96,3072]{1,0:T(8,128)}) %reduce-scatter.17.cloned.1.call-update) | async-done | bytes 1179664 | tf_op jit(solution)/shard_map/reduce_scatter | solution.py:279
  654.9 2.2 convert_element_type.257
  661.1 3.8 fusion.48
  665.0 0.8 copy-done.3
  666.0 38.6 %all-reduce.35 = (bf16[768]{0:T(1024)(128)(2,1)S(1)}, bf16[768]{0:T(1024)(128)(2,1)S(1)}, bf16[768]{0:T(1024)(128)(2,1)S(1)}, bf16[768]{0:T(1024)(128)(2,1)S(1)}...) all-reduce(f32[768]{0:T(1024)S(1)} %get-tuple-element.17, ...), channel_id=2, replica_groups=mesh['rep'=4,'shard'=8] {'shard'}, use_global_device_ids=true, to_apply=%region_11.0.clone | all-reduce | flops 9216 | bytes 55296
  705.3 6.4 all-reduce.38
  714.2 6.7 all-reduce.37
  725.6 95.5 %reduce-scatter.21.cloned.1.call-done = f32[384,768]{1,0:T(8,128)} async-done(((f32[3072,768]{1,0:T(8,128)}), f32[384,768]{1,0:T(8,128)}) %reduce-scatter.21.cloned.1.call-update) | async-done | bytes 1179664 | tf_op jit(solution)/shard_map/reduce_scatter | solution.py:281
  821.1 2.2 convert_element_type.261
  823.3 2.2 fusion.47
  825.5 4.4 fusion.34
  829.9 13.0 %reduce-scatter.15.cloned.1.call-done = bf16[24,768]{1,0:T(8,128)(2,1)} async-done(((bf16[96,768]{1,0:T(8,128)(2,1)}), bf16[24,768]{1,0:T(8,128)(2,1)}) %reduce-scatter.15.cloned.1.call-update) | async-done | bytes 36880 | tf_op jit(solution)/shard_map/reduce_scatter | solution.py:301
  842.9 5.7 all_gather.102
  849.3 17.1 %reduce-scatter.11.cloned.1.call-done = bf16[24,2304]{1,0:T(8,128)(2,1)} async-done(((bf16[96,2304]{1,0:T(8,128)(2,1)}), bf16[24,2304]{1,0:T(8,128)(2,1)}) %reduce-scatter.11.cloned.1.call-update) | async-done | bytes 110608 | tf_op jit(solution)/shard_map/reduce_scatter | solution.py:292
  866.3 6.5 all_gather.99
  872.8 1.0 convert_element_type.244
  873.8 17.8 %reduce-scatter.19.cloned.1.call-done = bf16[24,3072]{1,0:T(8,128)(2,1)} async-done(((bf16[96,3072]{1,0:T(8,128)(2,1)}), bf16[24,3072]{1,0:T(8,128)(2,1)}) %reduce-scatter.19.cloned.1.call-update) | async-done | bytes 147472 | tf_op jit(solution)/shard_map/reduce_scatter | solution.py:313
  891.5 7.1 all_gather.106
  898.7 1.1 convert_element_type.258
  899.8 16.2 %reduce-scatter.23.cloned.1.call-done = bf16[96,768]{1,0:T(8,128)(2,1)} async-done(((bf16[384,768]{1,0:T(8,128)(2,1)}), bf16[96,768]{1,0:T(8,128)(2,1)}) %reduce-scatter.23.cloned.1.call-update) | async-done | bytes 147472 | tf_op jit(solution)/shard_map/reduce_scatter | solution.py:319
  916.0 7.1 all_gather.108
  923.1 1.1 convert_element_type.262
  (123 shorter events, 14.2 us)
Async XLA Ops:
  7.2 80.9 %copy-start = (bf16[1,197,768]{2,1,0:T(8,128)(2,1)S(1)}, bf16[1,197,768]{2,1,0:T(8,128)(2,1)}, u32[]{:S(2)}) copy-start(bf16[1,197,768]{2,1,0:T(8,128)(2,1)} %param.16) | copy-start | bytes 907780
  7.2 81.2 %all-gather.6.cloned.1.call-start = ((), (), s32[]{:S(2)}) async-start(), calls=%async_computation.8 | async-start | bytes 3981312 | tf_op jit(solution)/shard_map/all_gather | solution.py:239
  7.9 112.5 %all-gather.8.cloned.1.call-start = ((), (), s32[]{:S(2)}) async-start(), calls=%async_computation.9 | async-start | bytes 1327104 | tf_op jit(solution)/shard_map/all_gather | solution.py:242
  8.7 192.0 %all-gather.10.cloned.1.call-start = ((), (), s32[]{:S(2)}) async-start(), calls=%async_computation.10 | async-start | bytes 5308416 | tf_op jit(solution)/shard_map/all_gather | solution.py:246
  9.4 271.1 %all-gather.12.cloned.1.call-start = ((), (), s32[]{:S(2)}) async-start(), calls=%async_computation.11 | async-start | bytes 5308416 | tf_op jit(solution)/shard_map/all_gather | solution.py:248
  10.0 348.1 %reduce-scatter.13.cloned.1.call-start = ((), (), s32[]{:S(2)}) async-start(), calls=%async_computation.14 | async-start | bytes 2654208 | tf_op jit(solution)/shard_map/reduce_scatter | solution.py:275
  95.2 1.7 copy-start.7
  96.9 23.6 %copy-start.4 = (f32[12,197,197]{1,2,0:T(8,128)}, f32[12,197,197]{1,2,0:T(8,128)S(1)}, u32[]{:S(2)}) copy-start(f32[12,197,197]{1,2,0:T(8,128)S(1)} %fusion.118) | copy-start | bytes 5588500
  99.2 101.5 %copy-start.5 = (bf16[12,64,197]{2,1,0:T(8,128)(2,1)}, bf16[12,64,197]{2,1,0:T(8,128)(2,1)S(1)}, u32[]{:S(2)}) copy-start(bf16[12,64,197]{2,1,0:T(8,128)(2,1)S(1)} %convolution_convert_fusion) | copy-start | bytes 907780
  280.5 4.4 copy-start.2
  284.8 1.8 copy-start.9
  284.8 2.0 copy-start.8
  286.7 1.4 copy-start.6
  287.2 0.8 copy-start.1
  289.9 200.1 %reduce-scatter.9.cloned.1.call-start = ((), (), s32[]{:S(2)}) async-start(), calls=%async_computation.12 | async-start | bytes 7962624 | tf_op jit(solution)/shard_map/reduce_scatter | solution.py:272
  322.7 332.2 %reduce-scatter.17.cloned.1.call-start = ((), (), s32[]{:S(2)}) async-start(), calls=%async_computation.16 | async-start | bytes 10616832 | tf_op jit(solution)/shard_map/reduce_scatter | solution.py:279
  329.3 491.8 %reduce-scatter.21.cloned.1.call-start = ((), (), s32[]{:S(2)}) async-start(), calls=%async_computation.18 | async-start | bytes 10616832 | tf_op jit(solution)/shard_map/reduce_scatter | solution.py:281
  334.9 507.9 %reduce-scatter.15.cloned.1.call-start = ((), (), s32[]{:S(2)}) async-start(), calls=%async_computation.15 | async-start | bytes 184320 | tf_op jit(solution)/shard_map/reduce_scatter | solution.py:301
  359.8 506.6 %reduce-scatter.11.cloned.1.call-start = ((), (), s32[]{:S(2)}) async-start(), calls=%async_computation.13 | async-start | bytes 552960 | tf_op jit(solution)/shard_map/reduce_scatter | solution.py:292
  492.0 399.5 %reduce-scatter.19.cloned.1.call-start = ((), (), s32[]{:S(2)}) async-start(), calls=%async_computation.17 | async-start | bytes 737280 | tf_op jit(solution)/shard_map/reduce_scatter | solution.py:313
  657.1 258.9 %reduce-scatter.23.cloned.1.call-start = ((), (), s32[]{:S(2)}) async-start(), calls=%async_computation.19 | async-start | bytes 737280 | tf_op jit(solution)/shard_map/reduce_scatter | solution.py:319
  665.0 0.8 copy-start.3
Sparse Core Ops, SparseCore 0:
  10.2 68.0 all-gather.5
  80.4 39.9 all-gather.7
  122.7 78.0 all-gather.9
  202.7 77.6 all-gather.11
  290.0 68.0 reduce-scatter.12
  361.6 128.3 reduce-scatter.8
  493.6 161.2 reduce-scatter.16
  658.5 162.5 reduce-scatter.20
  824.1 18.7 reduce-scatter.14
  845.2 21.0 reduce-scatter.10
  869.4 22.0 reduce-scatter.18
  893.9 22.0 reduce-scatter.22
where the time goes:
time: 932 us; the launch traced here: 931 us
  waiting for transfers between devices  654 us (70%)
  blocking collectives  145 us (16%)
  matrix products  71.3 us (8%)
  other arithmetic  21.1 us (2%)
  between operations  19.7 us (2%)
  local copies, waits for them, and re-layouts  19.4 us (2%)
    reduce_scatter x1, waiting for transfers between devices, per_device(): lax.psum_scatter(g09, 'shard', scatter_dimension=0, tiled=True)  163 us
    reduce_scatter x1, waiting for transfers between devices, per_device(): lax.psum_scatter(g02, 'shard', scatter_dimension=0, tiled=True)  130 us
    reduce_scatter x1, waiting for transfers between devices, per_device(): lax.psum_scatter(g11, 'shard', scatter_dimension=0, tiled=True)  95.5 us
    unnamed x4, blocking collectives  92 us
    all_gather x1, waiting for transfers between devices, per_device(): lax.all_gather(up_weight, 'shard', axis=0, tiled=True)  78.2 us
    all_gather x1, waiting for transfers between devices, per_device(): lax.all_gather(down_weight, 'shard', axis=0, tiled=True)  76.2 us
    all_gather x1, blocking collectives, per_device(): lax.all_gather(up_bias, 'shard', axis=0, tiled=True)  26.5 us
    dot_general x8, matrix products, matmul(): product = jnp.dot(flat, factor, preferred_element_type=jnp.float32)  25.5 us
  transfers between devices with their start and end apart: 12, of which 11 were waited for; matrix products, arithmetic and copies ran while one was open for 11% of the time, Pallas kernels for 0%

commit v1 on v0

--- a/solution.py
+++ b/solution.py
@@ -245,7 +245,9 @@
         lax.all_gather(second_bias, "shard", axis=0, tiled=True),
         lax.all_gather(up_weight, "shard", axis=0, tiled=True),
         lax.all_gather(up_bias, "shard", axis=0, tiled=True),
-        lax.all_gather(down_weight, "shard", axis=0, tiled=True),
+        jnp.concatenate(
+            lax.all_to_all(jnp.stack([down_weight] * lax.axis_size("shard")), "shard", 0, 0), axis=0
+        ),
         lax.all_gather(down_bias, "shard", axis=0, tiled=True),
     )
     output, saved = forward_pass(gathered, layer_input, live)

time: 932 us -> 1020 us (1.094)
  waiting for transfers between devices: 654 us -> 733 us
    reduce_scatter x1, waiting for transfers between devices: 130 us -> 191 us  [per_device(): lax.psum_scatter(g02, 'shard', scatter_dimension=0, tiled=True)]
    reduce_scatter x1, waiting for transfers between devices: 23.1 us -> 41.4 us  [per_device(): lax.psum_scatter(g05, 'shard', scatter_dimension=0, tiled=True)]
  transfers between devices with their start and end apart: 12 -> 13, of which waited for: 11 -> 11; matrix products, arithmetic and copies ran while one was open for 11% -> 10% of each run, Pallas kernels for 0% -> 0%
where the time goes in v1:
time: 1020 us
  waiting for transfers between devices  733 us (72%)
  blocking collectives  145 us (14%)
  matrix products  71.2 us (7%)
  local copies, waits for them, and re-layouts  22.9 us (2%)
  other arithmetic  21.1 us (2%)
  between operations  19.7 us (2%)
    reduce_scatter x1, waiting for transfers between devices, per_device(): lax.psum_scatter(g02, 'shard', scatter_dimension=0, tiled=True)  191 us
    reduce_scatter x1, waiting for transfers between devices, per_device(): lax.psum_scatter(g09, 'shard', scatter_dimension=0, tiled=True)  163 us
    reduce_scatter x1, waiting for transfers between devices, per_device(): lax.psum_scatter(g11, 'shard', scatter_dimension=0, tiled=True)  95.5 us
    unnamed x4, blocking collectives  92 us
    all_gather x1, waiting for transfers between devices, per_device(): lax.all_gather(up_weight, 'shard', axis=0, tiled=True)  78.2 us
    all_gather x1, waiting for transfers between devices, per_device(): lax.all_gather(down_weight, 'shard', axis=0, tiled=True)  76.2 us
    reduce_scatter x1, waiting for transfers between devices, per_device(): lax.psum_scatter(g05, 'shard', scatter_dimension=0, tiled=True)  41.4 us
    all_gather x1, blocking collectives, per_device(): lax.all_gather(up_bias, 'shard', axis=0, tiled=True)  26.5 us
  transfers between devices with their start and end apart: 13, of which 11 were waited for; matrix products, arithmetic and copies ran while one was open for 10% of the time, Pallas kernels for 0%

profile of v1, /device:TPU:0, one launch (start us, length us, event | category | flops | bytes accessed | tf_op | source)
XLA Modules:
  0.0 1018.3 jit_solution(12482183160917314412)
XLA Ops:
  10.0 1.3 fusion.110
  12.0 0.8 dynamic-update-slice.1
  12.9 0.8 dynamic-update-slice
  13.7 0.8 dynamic-update-slice.2
  14.6 0.8 dynamic-update-slice.3
  15.4 0.8 dynamic-update-slice.4
  16.2 0.8 dynamic-update-slice.7
  17.1 0.8 dynamic-update-slice.6
  17.9 0.8 dynamic-update-slice.5
  18.7 40.4 %all-reduce.36 = (bf16[768]{0:T(1024)(128)(2,1)S(1)}, bf16[768]{0:T(1024)(128)(2,1)S(1)}, bf16[768]{0:T(1024)(128)(2,1)S(1)}, bf16[768]{0:T(1024)(128)(2,1)S(1)}...) all-reduce(bf16[768]{0:T(1024)(128)(2,1)S(1)} %dynamic-update-slice, ...), channel_id=1, replica_groups=mesh['rep'=4,'shard'=8] {'shard'}, use_global_device_ids=true, to_apply=%add.1 | all-reduce | flops 6144 | bytes 24576
  60.5 26.5 %all-gather = bf16[8,1,384]{2,1,0:T(2,128)(2,1)S(1)} all-gather(bf16[1,1,384]{2,1,0:T(2,128)(2,1)S(1)} %reshape.380), channel_id=1, replica_groups=mesh['rep'=4,'shard'=8] {'shard'}, dimensions={0}, use_global_device_ids=true | all-gather | bytes 6912 | tf_op jit(solution)/shard_map/all_gather | solution.py:247
  87.0 1.1 convert_reduce_fusion
  88.4 3.0 convolution_bitcast_fusion
  92.2 0.9 copy.51
  93.1 0.9 copy.52
  94.0 1.1 copy.53
  95.2 1.7 fusion.118
  96.9 2.3 convolution_convert_fusion
  99.2 21.3 %all-gather.8.cloned.1.call-done = bf16[768,768]{1,0:T(8,128)(2,1)} async-done(((bf16[96,768]{1,0:T(8,128)(2,1)}), bf16[768,768]{1,0:T(8,128)(2,1)}) %all-gather.8.cloned.1.call-update) | async-done | bytes 1179664 | tf_op jit(solution)/shard_map/all_gather | solution.py:242
  120.5 1.8 fusion.112
  122.5 78.2 %all-gather.10.cloned.1.call-done = bf16[768,3072]{1,0:T(8,128)(2,1)} async-done(((bf16[96,3072]{1,0:T(8,128)(2,1)}), bf16[768,3072]{1,0:T(8,128)(2,1)}) %all-gather.10.cloned.1.call-update) | async-done | bytes 4718608 | tf_op jit(solution)/shard_map/all_gather | solution.py:246
  200.7 3.6 convolution_add_fusion
  204.3 76.2 %all-gather.12.cloned.1.call-done = bf16[3072,768]{1,0:T(8,128)(2,1)} async-done(((bf16[384,768]{1,0:T(8,128)(2,1)}), bf16[3072,768]{1,0:T(8,128)(2,1)}) %all-gather.12.cloned.1.call-update) | async-done | bytes 4718608 | tf_op jit(solution)/shard_map/all_gather | solution.py:266
  280.5 4.3 fusion.117
  284.9 1.8 fusion.52
  288.0 1.9 fusion.77
  290.1 3.9 fusion.6
  294.1 2.7 convolution_convert_fusion.1
  296.8 1.9 copy.55
  298.7 4.3 fusion.108
  303.0 3.1 fusion.119
  306.0 5.6 fusion.23
  311.6 5.5 fusion.109
  317.1 5.4 fusion.64
  322.6 6.5 fusion.56
  329.2 5.6 fusion.80
  334.9 3.5 stack.2
  338.3 4.6 all-to-all-start
  343.0 41.4 %reduce-scatter.13.cloned.1.call-done = f32[96,768]{1,0:T(8,128)} async-done(((f32[768,768]{1,0:T(8,128)}), f32[96,768]{1,0:T(8,128)}) %reduce-scatter.13.cloned.1.call-update) | async-done | bytes 294928 | tf_op jit(solution)/shard_map/reduce_scatter | solution.py:277
  384.4 1.6 convert_element_type.249
  386.1 191.1 %reduce-scatter.9.cloned.1.call-done = f32[96,2304]{1,0:T(8,128)} async-done(((f32[768,2304]{1,0:T(8,128)}), f32[96,2304]{1,0:T(8,128)}) %reduce-scatter.9.cloned.1.call-update) | async-done | bytes 884752 | tf_op jit(solution)/shard_map/reduce_scatter | solution.py:274
  577.2 2.0 convert_element_type.243
  579.2 162.8 %reduce-scatter.17.cloned.1.call-done = f32[96,3072]{1,0:T(8,128)} async-done(((f32[768,3072]{1,0:T(8,128)}), f32[96,3072]{1,0:T(8,128)}) %reduce-scatter.17.cloned.1.call-update) | async-done | bytes 1179664 | tf_op jit(solution)/shard_map/reduce_scatter | solution.py:281
  742.0 2.2 convert_element_type.257
  748.3 3.8 fusion.48
  752.2 0.8 copy-done.3
  753.1 38.6 %all-reduce.35 = (bf16[768]{0:T(1024)(128)(2,1)S(1)}, bf16[768]{0:T(1024)(128)(2,1)S(1)}, bf16[768]{0:T(1024)(128)(2,1)S(1)}, bf16[768]{0:T(1024)(128)(2,1)S(1)}...) all-reduce(f32[768]{0:T(1024)S(1)} %get-tuple-element.17, ...), channel_id=2, replica_groups=mesh['rep'=4,'shard'=8] {'shard'}, use_global_device_ids=true, to_apply=%region_11.0.clone | all-reduce | flops 9216 | bytes 55296
  792.5 6.4 all-reduce.38
  801.4 6.6 all-reduce.37
  812.8 95.5 %reduce-scatter.21.cloned.1.call-done = f32[384,768]{1,0:T(8,128)} async-done(((f32[3072,768]{1,0:T(8,128)}), f32[384,768]{1,0:T(8,128)}) %reduce-scatter.21.cloned.1.call-update) | async-done | bytes 1179664 | tf_op jit(solution)/shard_map/reduce_scatter | solution.py:283
  908.2 2.1 convert_element_type.261
  910.4 2.2 fusion.47
  912.6 4.4 fusion.34
  917.0 13.1 %reduce-scatter.15.cloned.1.call-done = bf16[24,768]{1,0:T(8,128)(2,1)} async-done(((bf16[96,768]{1,0:T(8,128)(2,1)}), bf16[24,768]{1,0:T(8,128)(2,1)}) %reduce-scatter.15.cloned.1.call-update) | async-done | bytes 36880 | tf_op jit(solution)/shard_map/reduce_scatter | solution.py:303
  930.1 5.7 all_gather.101
  936.5 17.1 %reduce-scatter.11.cloned.1.call-done = bf16[24,2304]{1,0:T(8,128)(2,1)} async-done(((bf16[96,2304]{1,0:T(8,128)(2,1)}), bf16[24,2304]{1,0:T(8,128)(2,1)}) %reduce-scatter.11.cloned.1.call-update) | async-done | bytes 110608 | tf_op jit(solution)/shard_map/reduce_scatter | solution.py:294
  953.6 6.5 all_gather.98
  960.0 1.0 convert_element_type.244
  961.0 17.7 %reduce-scatter.19.cloned.1.call-done = bf16[24,3072]{1,0:T(8,128)(2,1)} async-done(((bf16[96,3072]{1,0:T(8,128)(2,1)}), bf16[24,3072]{1,0:T(8,128)(2,1)}) %reduce-scatter.19.cloned.1.call-update) | async-done | bytes 147472 | tf_op jit(solution)/shard_map/reduce_scatter | solution.py:315
  978.7 7.1 all_gather.105
  985.9 1.1 convert_element_type.258
  987.0 16.2 %reduce-scatter.23.cloned.1.call-done = bf16[96,768]{1,0:T(8,128)(2,1)} async-done(((bf16[384,768]{1,0:T(8,128)(2,1)}), bf16[96,768]{1,0:T(8,128)(2,1)}) %reduce-scatter.23.cloned.1.call-update) | async-done | bytes 147472 | tf_op jit(solution)/shard_map/reduce_scatter | solution.py:321
  1003.2 7.1 all_gather.107
  1010.3 1.1 convert_element_type.262
  (126 shorter events, 15.8 us)
Async XLA Ops:
  7.2 80.9 %copy-start = (bf16[1,197,768]{2,1,0:T(8,128)(2,1)S(1)}, bf16[1,197,768]{2,1,0:T(8,128)(2,1)}, u32[]{:S(2)}) copy-start(bf16[1,197,768]{2,1,0:T(8,128)(2,1)} %param.16) | copy-start | bytes 907780
  7.2 81.2 %all-gather.6.cloned.1.call-start = ((), (), s32[]{:S(2)}) async-start(), calls=%async_computation.9 | async-start | bytes 3981312 | tf_op jit(solution)/shard_map/all_gather | solution.py:239
  7.9 112.5 %all-gather.8.cloned.1.call-start = ((), (), s32[]{:S(2)}) async-start(), calls=%async_computation.10 | async-start | bytes 1327104 | tf_op jit(solution)/shard_map/all_gather | solution.py:242
  8.7 192.0 %all-gather.10.cloned.1.call-start = ((), (), s32[]{:S(2)}) async-start(), calls=%async_computation.11 | async-start | bytes 5308416 | tf_op jit(solution)/shard_map/all_gather | solution.py:246
  9.4 271.1 %all-gather.12.cloned.1.call-start = ((), (), s32[]{:S(2)}) async-start(), calls=%async_computation.12 | async-start | bytes 5308416 | tf_op jit(solution)/shard_map/all_gather | solution.py:266
  10.0 374.4 %reduce-scatter.13.cloned.1.call-start = ((), (), s32[]{:S(2)}) async-start(), calls=%async_computation.15 | async-start | bytes 2654208 | tf_op jit(solution)/shard_map/reduce_scatter | solution.py:277
  95.2 1.7 copy-start.7
  96.9 23.6 %copy-start.4 = (f32[12,197,197]{1,2,0:T(8,128)}, f32[12,197,197]{1,2,0:T(8,128)S(1)}, u32[]{:S(2)}) copy-start(f32[12,197,197]{1,2,0:T(8,128)S(1)} %fusion.118) | copy-start | bytes 5588500
  99.2 101.5 %copy-start.5 = (bf16[12,64,197]{2,1,0:T(8,128)(2,1)}, bf16[12,64,197]{2,1,0:T(8,128)(2,1)S(1)}, u32[]{:S(2)}) copy-start(bf16[12,64,197]{2,1,0:T(8,128)(2,1)S(1)} %convolution_convert_fusion) | copy-start | bytes 907780
  280.5 4.4 copy-start.2
  284.8 1.8 copy-start.9
  284.8 2.0 copy-start.8
  286.7 1.4 copy-start.6
  287.2 0.8 copy-start.1
  289.9 287.3 %reduce-scatter.9.cloned.1.call-start = ((), (), s32[]{:S(2)}) async-start(), calls=%async_computation.13 | async-start | bytes 7962624 | tf_op jit(solution)/shard_map/reduce_scatter | solution.py:274
  322.6 419.5 %reduce-scatter.17.cloned.1.call-start = ((), (), s32[]{:S(2)}) async-start(), calls=%async_computation.17 | async-start | bytes 10616832 | tf_op jit(solution)/shard_map/reduce_scatter | solution.py:281
  329.2 579.0 %reduce-scatter.21.cloned.1.call-start = ((), (), s32[]{:S(2)}) async-start(), calls=%async_computation.19 | async-start | bytes 10616832 | tf_op jit(solution)/shard_map/reduce_scatter | solution.py:283
  338.3 574.3 %all-to-all-start = ((bf16[8,384,768]{2,1,0:T(8,128)(2,1)}), bf16[8,384,768]{2,1,0:T(8,128)(2,1)}, u32[]{:S(2)}, u32[]{:S(2)}) async-start(bf16[8,384,768]{2,1,0:T(8,128)(2,1)} %stack.2), calls=%async_computation | async-start | bytes 9437184 | tf_op jit(solution)/shard_map/all_to_all | solution.py:249
  343.0 587.1 %reduce-scatter.15.cloned.1.call-start = ((), (), s32[]{:S(2)}) async-start(), calls=%async_computation.16 | async-start | bytes 184320 | tf_op jit(solution)/shard_map/reduce_scatter | solution.py:303
  386.0 567.5 %reduce-scatter.11.cloned.1.call-start = ((), (), s32[]{:S(2)}) async-start(), calls=%async_computation.14 | async-start | bytes 552960 | tf_op jit(solution)/shard_map/reduce_scatter | solution.py:294
  579.2 399.6 %reduce-scatter.19.cloned.1.call-start = ((), (), s32[]{:S(2)}) async-start(), calls=%async_computation.18 | async-start | bytes 737280 | tf_op jit(solution)/shard_map/reduce_scatter | solution.py:315
  744.2 259.0 %reduce-scatter.23.cloned.1.call-start = ((), (), s32[]{:S(2)}) async-start(), calls=%async_computation.20 | async-start | bytes 737280 | tf_op jit(solution)/shard_map/reduce_scatter | solution.py:321
  752.2 0.8 copy-start.3
Sparse Core Ops, SparseCore 0:
  10.2 68.0 all-gather.5
  80.4 39.9 all-gather.7
  122.7 78.0 all-gather.9
  202.7 77.6 all-gather.11
  290.0 94.3 reduce-scatter.12
  387.9 189.2 reduce-scatter.8
  580.7 161.2 reduce-scatter.16
  745.6 162.5 reduce-scatter.20
  911.2 18.8 reduce-scatter.14
  932.4 21.0 reduce-scatter.10
  956.6 22.0 reduce-scatter.18
  981.1 22.0 reduce-scatter.22
